TPU v7x, 32 devices: a whole 2x2x4 slice. The times are simulated.
32 devices in a mesh: dom: 8 (over z, x), ens: 4 (over y, core).
Axes of the slice: x: 2, y: 2, z: 4, core: 2. Of those that a mesh axis runs over, the one named last changes fastest.
Arguments:
- link_flow: float32 [64, 16384], P('ens', 'dom'), may hold values from 0.2 to 1
- free_time: float32 [16384], P('dom'), may hold values from 0.1 to 4
- capacity: float32 [16384], P('dom'), may hold values from 0.5 to 1.5
- demand: float32 [64, 8, 256], P('ens', 'dom'), may hold values from 0.05 to 0.3
- path_od: int32 [8, 1024], P('dom'), may hold values from 0 to 255, never falling along the last dimension, each value on 1 to 8 neighbouring positions
- send_blocks: int32 [8, 8, 4], P('dom'), may hold values from 0 to 15
- send_counts: int32 [8, 8], P('dom'), may hold values from 0 to 4, as said below
- tile_links: int32 [8, 8, 4, 4, 128], P('dom'), may hold values from -128 to 127
- tile_paths: int32 [8, 8, 4], P('dom'), may hold values from 0 to 7
Outputs:
- link_load: float32 [64, 16384], P('ens', 'dom')
- path_flow: float32 [64, 8192], P('ens', 'dom')
- mean_time: float32 [16384], P('dom')
Inputs may be any that keep to these rules, and one draw needn't show every extreme that they name: `path_od`: each row holds non-decreasing pair ids; every id of 0 .. 255 names 1 to 8 paths of its row. `send_counts`: some path owner receives 4 live tiles from every link partition.
All inputs are finite; a program needn't handle non-finite values.
Results may differ from a plain program's by a relative error of at most 0.0003.
Values sent between devices are 32-bit elements; how exact they have to be, the bound alone decides.
A program may use at most 64 MiB of HBM per device.

v0:
```python
import jax
import jax.numpy as jnp
from jax import lax
from jax.sharding import PartitionSpec as P

ITERS = 2


dispersion = 2.0
tile_group = 8


def bpr_times(current, free_time, capacity):
    loading = current / capacity
    square = loading * loading
    return free_time * (1.0 + 0.15 * square * square)


def link_path_incidence(link_rows):
    positions = jnp.arange(link_rows.shape[-1], dtype=jnp.int32)
    return jnp.sum(
        (link_rows[:, :, None, :] == positions[None, None, :, None]).astype(jnp.float32), axis=1
    )


def logit_split(path_cost, anchor_dest, demands):
    pair_count = demands.shape[1]
    lowest = (
        jnp.full((path_cost.shape[0], pair_count), jnp.inf, path_cost.dtype)
        .at[:, anchor_dest]
        .min(path_cost)
    )
    weight = jnp.exp(-dispersion * (path_cost - lowest[:, anchor_dest]))
    weight_sum = (
        jnp.zeros((path_cost.shape[0], pair_count), path_cost.dtype).at[:, anchor_dest].add(weight)
    )
    return demands[:, anchor_dest] * weight / weight_sum[:, anchor_dest]


def deliver(buffer):
    return lax.all_to_all(buffer, "dom", split_axis=0, concat_axis=0, tiled=True)


def local(
    link_flow,
    free_time,
    capacity,
    demand,
    path_od,
    send_blocks,
    send_counts,
    tile_links,
    tile_paths,
):
    scenarios = link_flow.shape[0]
    block_width = tile_links.shape[-1]
    hop_count = tile_links.shape[3]
    slot_count = send_blocks.shape[2]
    tile_count = send_blocks.shape[1] * slot_count
    group_count = tile_count // tile_group
    link_blocks = free_time.shape[0] // block_width
    path_blocks = path_od.shape[1] // block_width
    slot_ids = jnp.arange(slot_count, dtype=jnp.int32)
    live_mask = (
        (slot_ids[None, :] < send_counts[0][:, None]).astype(jnp.float32).reshape(tile_count)
    )
    blocks = send_blocks[0].reshape(tile_count)
    path_block = tile_paths[0].reshape(tile_count)
    link_rows = tile_links[0].reshape(group_count, tile_group, hop_count, block_width)
    path_pick = (path_block[:, None] == jnp.arange(path_blocks, dtype=jnp.int32)[None, :]).astype(
        jnp.float32
    )
    path_pick = path_pick.reshape(group_count, tile_group, path_blocks)
    choose = (blocks[:, None] == jnp.arange(link_blocks, dtype=jnp.int32)[None, :]).astype(
        jnp.float32
    ) * live_mask[:, None]
    anchor_dest = path_od[0]
    demands = demand[:, 0, :]
    current = link_flow
    path_flow = None
    for iteration in range(ITERS):
        link_times = bpr_times(current, free_time, capacity).reshape(
            scenarios, link_blocks, block_width
        )
        link_times = jnp.transpose(link_times, (1, 0, 2))
        outgoing = jnp.take(link_times, blocks, axis=0) * live_mask[:, None, None]
        incoming = deliver(outgoing).reshape(group_count, tile_group, scenarios, block_width)

        def add_cost(running, payload):
            section_travel_times, grouped_path_rows, selector = payload
            one_hot_selector = link_path_incidence(grouped_path_rows)
            partial_link_value = jnp.einsum(
                "dwi,dih->dwh",
                section_travel_times,
                one_hot_selector,
                precision=lax.Precision.HIGHEST,
            )
            return (
                running
                + jnp.einsum(
                    "tsp,tb->bsp", partial_link_value, selector, precision=lax.Precision.HIGHEST
                ),
                None,
            )

        initial = jnp.zeros((path_blocks, scenarios, block_width), jnp.float32)
        path_cost, _ = lax.scan(add_cost, initial, (incoming, link_rows, path_pick))
        path_cost = jnp.transpose(path_cost, (1, 0, 2)).reshape(
            scenarios, path_blocks * block_width
        )
        path_flow = logit_split(path_cost, anchor_dest, demands)
        path_major = jnp.transpose(
            path_flow.reshape(scenarios, path_blocks, block_width), (1, 0, 2)
        )
        section_flow = jnp.take(path_major, path_block, axis=0).reshape(
            group_count, tile_group, scenarios, block_width
        )

        def spread(payload):
            grouped_path_flow, grouped_path_rows = payload
            return jnp.einsum(
                "zdo,zmo->zdm",
                grouped_path_flow,
                link_path_incidence(grouped_path_rows),
                precision=lax.Precision.HIGHEST,
            )

        loaded_link_flow = lax.map(spread, (section_flow, link_rows)).reshape(
            tile_count, scenarios, block_width
        )
        returned = deliver(loaded_link_flow)
        auxiliary = jnp.einsum("nsl,nb->bsl", returned, choose, precision=lax.Precision.HIGHEST)
        auxiliary = jnp.transpose(auxiliary, (1, 0, 2)).reshape(
            scenarios, link_blocks * block_width
        )
        current = current + (auxiliary - current) / (iteration + 2.0)
    final_times = jnp.sum(bpr_times(current, free_time, capacity), axis=0)
    mean_time = lax.psum(final_times, "ens") / (scenarios * lax.axis_size("ens"))
    return (current, path_flow, mean_time)


def solution(mesh):
    in_specs = (
        P("ens", "dom"),
        P("dom"),
        P("dom"),
        P("ens", "dom", None),
        P("dom", None),
        P("dom", None, None),
        P("dom", None),
        P("dom", None, None, None, None),
        P("dom", None, None),
    )
    out_specs = (P("ens", "dom"), P("ens", "dom"), P("dom"))
    return jax.shard_map(local, mesh=mesh, in_specs=in_specs, out_specs=out_specs, check_vma=False)
```

profile of v0, /device:TPU:0, one launch (start us, length us, event | category | flops | bytes accessed | tf_op | source)
XLA Modules:
  0.0 129.0 jit_solution(3030443439453062055)
XLA Ops:
  2.3 1.0 bitcast_bitcast_fusion.1
  3.9 0.8 select_multiply_fusion.1
  4.7 7.3 %all-to-all-start = ((f32[32,16,128]{2,1,0:T(8,128)}), f32[32,16,128]{2,1,0:T(8,128)S(1)}, u32[]{:S(2)}, u32[]{:S(2)}) async-start(f32[32,16,128]{2,1,0:T(8,128)} %select_multiply_fusion.1), calls=%async_computation | async-start | bytes 524288 | tf_op jit(solution)/shard_map/all_to_all | solution.py:41
  12.4 2.8 %gather_fusion = f32[1024,16]{1,0:T(8,128)S(1)} fusion(f32[16,256]{0,1:T(8,128)S(1)} %bitcast.203, s32[1024]{0:T(1024)S(1)} %broadcast_clamp_fusion), kind=kCustom, calls=%fused_computation.4 | custom fusion | bytes 135168 | tf_op jit(solution)/shard_map/gather | solution.py:37
  15.5 5.4 %all-to-all-done = f32[32,16,128]{2,1,0:T(8,128)S(1)} async-done(((f32[32,16,128]{2,1,0:T(8,128)}), f32[32,16,128]{2,1,0:T(8,128)S(1)}, u32[]{:S(2)}, u32[]{:S(2)}) %all-to-all-start) | async-done | bytes 262176 | tf_op jit(solution)/shard_map/all_to_all | solution.py:41
  20.9 4.6 %while.44 = (s32[]{:T(128)}, f32[8,16,128]{2,0,1:T(8,128)S(1)}, f32[4,8,8]{2,1,0:T(8,128)S(1)}, f32[4,8,16,128]{3,2,1,0:T(8,128)S(1)}, s32[4,8,4,128]{3,2,1,0:T(4,128)S(1)}, /*index=5*/s32[]{:T(128)}, s32[]{:T(128)}) while((s32[]{:T(128)}, f32[8,16,128]{2,0,1:T(8,128)S(1)}, f32[4,8,8]{2,1,0:T(8,128)S(1)}, ...), condition=%wide.region_2.4_spmd.clone, body=%wide.region_0.3_spmd.clone.sunk | while | flops 28213248 | bytes 1429603 | solution.py:107
  25.7 6.5 %scatter_custom_fusion = f32[16,256]{0,1:T(8,128)S(1)} fusion(s32[1024]{0:T(1024)S(1)} %bitcast.224, f32[1024,16]{1,0:T(8,128)S(1)} %bitcast.211, f32[]{:T(128)} %constant.87.clone.1), kind=kCustom, calls=%fused_computation.110 | custom fusion | flops 16384 | bytes 16388 | tf_op jit(solution)/shard_map/scatter-min | solution.py:31
  32.2 2.8 %gather_fusion.1 = f32[1024,16]{1,0:T(8,128)S(1)} fusion(f32[16,256]{0,1:T(8,128)S(1)} %scatter_custom_fusion, s32[1024]{0:T(1024)S(1)} %broadcast_clamp_fusion), kind=kCustom, calls=%fused_computation.5 | custom fusion | bytes 135168 | tf_op jit(solution)/shard_map/gather | solution.py:33
  35.0 6.6 %scatter_custom_fusion.1 = f32[16,256]{0,1:T(8,128)S(1)} fusion(s32[1024]{0:T(1024)S(1)} %bitcast.225, f32[16,1024]{0,1:T(8,128)S(1)} %bitcast.212, f32[1024,16]{1,0:T(8,128)S(1)} %gather_fusion.1, f32[]{:T(128)} %constant.88.clone.1, f32[]{:T(128)} %constant.65.clone.1), kind=kCustom, calls=%fused_computation.59 | custom fusion | flops 49152 | bytes 1064968 | tf_op jit(solution)/shard_map/scatter-add | solution.py:35
  41.6 2.8 %gather_fusion.2 = f32[1024,16]{1,0:T(8,128)S(1)} fusion(f32[16,256]{0,1:T(8,128)S(1)} %scatter_custom_fusion.1, s32[1024]{0:T(1024)S(1)} %broadcast_clamp_fusion), kind=kCustom, calls=%fused_computation.6 | custom fusion | bytes 135168 | tf_op jit(solution)/shard_map/gather | solution.py:37
  45.5 5.0 %while.42 = (s32[]{:T(128)}, f32[4,8,16,128]{3,2,1,0:T(8,128)S(1)}, f32[4,8,16,128]{3,2,1,0:T(8,128)S(1)}, s32[4,8,4,128]{3,2,1,0:T(4,128)S(1)}, s32[]{:T(128)}) while((s32[]{:T(128)}, f32[4,8,16,128]{3,2,1,0:T(8,128)S(1)}, f32[4,8,16,128]{3,2,1,0:T(8,128)S(1)}, s32[4,8,4,128]{3,2,1,0:T(4,128)S(1)}, s32[]{:T(128)}) %tuple.96), condition=%wide.region_7.10_spmd, body=%wide.region_5.9_spmd.sunk | while | flops 26607616 | bytes 1229889 | solution.py:128
  45.9 0.9 fusion.106
  47.1 0.9 fusion.106
  48.3 0.9 fusion.106
  49.6 0.9 fusion.106
  50.5 12.1 %all_to_all.20 = f32[32,16,128]{2,1,0:T(8,128)S(1)} all-to-all(f32[32,16,128]{2,1,0:T(8,128)S(1)} %bitcast.220), channel_id=1, replica_groups=mesh['dom'=8,'ens'=4] {'dom'}, dimensions={0} | all-to-all | bytes 524288 | tf_op jit(solution)/shard_map/all_to_all | solution.py:41
  63.6 0.8 select_multiply_fusion
  64.5 3.6 %all-to-all-start.2 = ((f32[32,16,128]{2,1,0:T(8,128)}), f32[32,16,128]{2,1,0:T(8,128)S(1)}, u32[]{:S(2)}, u32[]{:S(2)}) async-start(f32[32,16,128]{2,1,0:T(8,128)} %select_multiply_fusion), calls=%async_computation.2 | async-start | bytes 524288 | tf_op jit(solution)/shard_map/all_to_all | solution.py:41
  68.1 8.5 %all-to-all-done.2 = f32[32,16,128]{2,1,0:T(8,128)S(1)} async-done(((f32[32,16,128]{2,1,0:T(8,128)}), f32[32,16,128]{2,1,0:T(8,128)S(1)}, u32[]{:S(2)}, u32[]{:S(2)}) %all-to-all-start.2) | async-done | bytes 262176 | tf_op jit(solution)/shard_map/all_to_all | solution.py:41
  76.6 4.6 %while.45 = (s32[]{:T(128)}, f32[8,16,128]{2,0,1:T(8,128)S(1)}, f32[4,8,8]{2,1,0:T(8,128)S(1)}, f32[4,8,16,128]{3,2,1,0:T(8,128)S(1)}, s32[4,8,4,128]{3,2,1,0:T(4,128)S(1)}, /*index=5*/s32[]{:T(128)}, s32[]{:T(128)}) while((s32[]{:T(128)}, f32[8,16,128]{2,0,1:T(8,128)S(1)}, f32[4,8,8]{2,1,0:T(8,128)S(1)}, ...), condition=%wide.region_10.13_spmd.clone, body=%wide.region_8.12_spmd.clone.sunk | while | flops 28213248 | bytes 1429603 | solution.py:107
  81.4 6.6 %scatter_custom_fusion.2 = f32[16,256]{0,1:T(8,128)S(1)} fusion(s32[1024]{0:T(1024)S(1)} %bitcast.226, f32[1024,16]{1,0:T(8,128)S(1)} %bitcast.210, f32[]{:T(128)} %constant.87.clone.1), kind=kCustom, calls=%fused_computation.108 | custom fusion | flops 16384 | bytes 16388 | tf_op jit(solution)/shard_map/scatter-min | solution.py:31
  88.0 2.8 %gather_fusion.3 = f32[1024,16]{1,0:T(8,128)S(1)} fusion(f32[16,256]{0,1:T(8,128)S(1)} %scatter_custom_fusion.2, s32[1024]{0:T(1024)S(1)} %broadcast_clamp_fusion), kind=kCustom, calls=%fused_computation.7 | custom fusion | bytes 135168 | tf_op jit(solution)/shard_map/gather | solution.py:33
  91.0 6.5 %scatter_custom_fusion.3 = f32[16,256]{0,1:T(8,128)S(1)} fusion(s32[1024]{0:T(1024)S(1)} %bitcast.227, f32[16,1024]{0,1:T(8,128)S(1)} %fusion.27, f32[]{:T(128)} %constant.65.clone.1), kind=kCustom, calls=%fused_computation.54 | custom fusion | flops 16384 | bytes 540676 | tf_op jit(solution)/shard_map/scatter-add | solution.py:35
  97.5 2.8 %gather_fusion.4 = f32[1024,16]{1,0:T(8,128)S(1)} fusion(f32[16,256]{0,1:T(8,128)S(1)} %scatter_custom_fusion.3, s32[1024]{0:T(1024)S(1)} %broadcast_clamp_fusion), kind=kCustom, calls=%fused_computation.8 | custom fusion | bytes 135168 | tf_op jit(solution)/shard_map/gather | solution.py:37
  102.1 7.4 %while.43 = (s32[]{:T(128)}, f32[4,8,16,128]{3,2,1,0:T(8,128)}, f32[4,8,16,128]{3,2,1,0:T(8,128)S(1)}, s32[4,8,4,128]{3,2,1,0:T(4,128)S(1)}, s32[]{:T(128)}) while((s32[]{:T(128)}, f32[4,8,16,128]{3,2,1,0:T(8,128)}, f32[4,8,16,128]{3,2,1,0:T(8,128)S(1)}, s32[4,8,4,128]{3,2,1,0:T(4,128)S(1)}, s32[]{:T(128)}) %tuple.95), condition=%wide.region_15.18_spmd, body=%wide.region_13.17_spmd.sunk | while | flops 26607616 | bytes 1229889 | solution.py:128
  102.4 1.6 %fusion.109 = f32[4,8,16,128]{3,2,1,0:T(8,128)} fusion(f32[4,8,16,128]{3,2,1,0:T(8,128)} %get-tuple-element.379, s32[]{:T(128)} %get-tuple-element.378, f32[8,128,128]{2,1,0:T(8,128)S(1)} %convert_reduce_fusion.9, f32[4,8,16,128]{3,2,1,0:T(8,128)S(1)} %get-tuple-element.385), kind=kOutput, calls=%fused_computation.24.clone.1 | convolution fusion | flops 25165824 | bytes 656384 | tf_op jit(solution)/shard_map/while/body/eval_jaxpr/zdo,zmo->zdm/dot_general | solution.py:121
  104.2 1.5 %fusion.109 = f32[4,8,16,128]{3,2,1,0:T(8,128)} fusion(f32[4,8,16,128]{3,2,1,0:T(8,128)} %get-tuple-element.379, s32[]{:T(128)} %get-tuple-element.378, f32[8,128,128]{2,1,0:T(8,128)S(1)} %convert_reduce_fusion.9, f32[4,8,16,128]{3,2,1,0:T(8,128)S(1)} %get-tuple-element.385), kind=kOutput, calls=%fused_computation.24.clone.1 | convolution fusion | flops 25165824 | bytes 656384 | tf_op jit(solution)/shard_map/while/body/eval_jaxpr/zdo,zmo->zdm/dot_general | solution.py:121
  106.1 1.6 %fusion.109 = f32[4,8,16,128]{3,2,1,0:T(8,128)} fusion(f32[4,8,16,128]{3,2,1,0:T(8,128)} %get-tuple-element.379, s32[]{:T(128)} %get-tuple-element.378, f32[8,128,128]{2,1,0:T(8,128)S(1)} %convert_reduce_fusion.9, f32[4,8,16,128]{3,2,1,0:T(8,128)S(1)} %get-tuple-element.385), kind=kOutput, calls=%fused_computation.24.clone.1 | convolution fusion | flops 25165824 | bytes 656384 | tf_op jit(solution)/shard_map/while/body/eval_jaxpr/zdo,zmo->zdm/dot_general | solution.py:121
  108.0 1.5 %fusion.109 = f32[4,8,16,128]{3,2,1,0:T(8,128)} fusion(f32[4,8,16,128]{3,2,1,0:T(8,128)} %get-tuple-element.379, s32[]{:T(128)} %get-tuple-element.378, f32[8,128,128]{2,1,0:T(8,128)S(1)} %convert_reduce_fusion.9, f32[4,8,16,128]{3,2,1,0:T(8,128)S(1)} %get-tuple-element.385), kind=kOutput, calls=%fused_computation.24.clone.1 | convolution fusion | flops 25165824 | bytes 656384 | tf_op jit(solution)/shard_map/while/body/eval_jaxpr/zdo,zmo->zdm/dot_general | solution.py:121
  109.5 3.5 %all-to-all-start.3 = ((f32[32,16,128]{2,1,0:T(8,128)}), f32[32,16,128]{2,1,0:T(8,128)S(1)}, u32[]{:S(2)}, u32[]{:S(2)}) async-start(f32[32,16,128]{2,1,0:T(8,128)} %bitcast.43), calls=%async_computation.3 | async-start | bytes 524288 | tf_op jit(solution)/shard_map/all_to_all | solution.py:41
  113.9 7.6 %all-to-all-done.3 = f32[32,16,128]{2,1,0:T(8,128)S(1)} async-done(((f32[32,16,128]{2,1,0:T(8,128)}), f32[32,16,128]{2,1,0:T(8,128)S(1)}, u32[]{:S(2)}, u32[]{:S(2)}) %all-to-all-start.3) | async-done | bytes 262176 | tf_op jit(solution)/shard_map/all_to_all | solution.py:41
  122.7 5.7 %psum.7 = f32[2048]{0:T(1024)S(1)} all-reduce(f32[2048]{0:T(1024)S(1)} %get-tuple-element.202), channel_id=1, replica_groups=mesh['dom'=8,'ens'=4] {'ens'}, use_global_device_ids=true, to_apply=%region_17.20 | all-reduce | flops 2048 | bytes 16384 | tf_op jit(solution)/shard_map/psum | solution.py:138
  (106 shorter events, 21.2 us)
Async XLA Ops:
  3.9 8.2 %copy-start.6 = (s32[1,8,4]{1,2,0:T(4,128)S(1)}, s32[1,8,4]{1,2,0:T(4,128)}, u32[]{:S(2)}) copy-start(s32[1,8,4]{1,2,0:T(4,128)} %param.29) | copy-start | bytes 388
  3.9 8.2 %copy-start.5 = (s32[1,1024]{1,0:T(1,128)S(1)}, s32[1,1024]{1,0:T(1,128)}, u32[]{:S(2)}) copy-start(s32[1,1024]{1,0:T(1,128)} %param.25) | copy-start | bytes 12292
  3.9 8.4 %copy-start.4 = (f32[16,1,256]{2,1,0:T(1,128)S(1)}, f32[16,1,256]{2,1,0:T(1,128)}, u32[]{:S(2)}) copy-start(f32[16,1,256]{2,1,0:T(1,128)} %param.24) | copy-start | bytes 49156
  4.7 16.2 %all-to-all-start = ((f32[32,16,128]{2,1,0:T(8,128)}), f32[32,16,128]{2,1,0:T(8,128)S(1)}, u32[]{:S(2)}, u32[]{:S(2)}) async-start(f32[32,16,128]{2,1,0:T(8,128)} %select_multiply_fusion.1), calls=%async_computation | async-start | bytes 524288 | tf_op jit(solution)/shard_map/all_to_all | solution.py:41
  12.4 8.5 %copy-start = (s32[1,8,4,4,128]{4,3,2,1,0:T(4,128)S(1)}, s32[1,8,4,4,128]{4,3,2,1,0:T(4,128)}, u32[]{:S(2)}) copy-start(s32[1,8,4,4,128]{4,3,2,1,0:T(4,128)} %param.28) | copy-start | bytes 196612
  50.5 12.4 %copy-start.1 = (f32[16,2048]{1,0:T(8,128)S(1)}, f32[16,2048]{1,0:T(8,128)}, u32[]{:S(2)}) copy-start(f32[16,2048]{1,0:T(8,128)} %param.21) | copy-start | bytes 393220
  50.5 12.5 %copy-start.2 = (f32[2048]{0:T(1024)S(1)}, f32[2048]{0:T(1024)}, u32[]{:S(2)}) copy-start(f32[2048]{0:T(1024)} %param.23) | copy-start | bytes 24580
  50.5 12.5 %copy-start.3 = (f32[2048]{0:T(1024)S(1)}, f32[2048]{0:T(1024)}, u32[]{:S(2)}) copy-start(f32[2048]{0:T(1024)} %param.22) | copy-start | bytes 24580
  64.5 12.1 %all-to-all-start.2 = ((f32[32,16,128]{2,1,0:T(8,128)}), f32[32,16,128]{2,1,0:T(8,128)S(1)}, u32[]{:S(2)}, u32[]{:S(2)}) async-start(f32[32,16,128]{2,1,0:T(8,128)} %select_multiply_fusion), calls=%async_computation.2 | async-start | bytes 524288 | tf_op jit(solution)/shard_map/all_to_all | solution.py:41
  109.5 12.1 %all-to-all-start.3 = ((f32[32,16,128]{2,1,0:T(8,128)}), f32[32,16,128]{2,1,0:T(8,128)S(1)}, u32[]{:S(2)}, u32[]{:S(2)}) async-start(f32[32,16,128]{2,1,0:T(8,128)} %bitcast.43), calls=%async_computation.3 | async-start | bytes 524288 | tf_op jit(solution)/shard_map/all_to_all | solution.py:41
where the time goes:
time: 130 us; the launch traced here: 129 us
  other arithmetic  36.4 us (28%)
  waiting for transfers between devices  21.6 us (17%)
  local copies, waits for them, and re-layouts  20.5 us (16%)
  blocking collectives  17.8 us (14%)
  matrix products  17 us (13%)
  starting transfers between devices  14.4 us (11%)
    all_to_all x3, waiting for transfers between devices, deliver(): lax.all_to_all(buffer, 'dom', split_axis=0, concat_axis=0, tiled=True)  21.6 us
    all_to_all x3, starting transfers between devices, deliver(): lax.all_to_all(buffer, 'dom', split_axis=0, concat_axis=0, tiled=True)  14.4 us
    another operation x2, other arithmetic, logit_split(): lowest = jnp.full((path_cost.shape[0], pair_count), jnp.inf, path_cost.dt...  13.1 us
    scatter-add x2, other arithmetic, logit_split(): jnp.zeros((path_cost.shape[0], pair_count), path_cost.dtype)  13.1 us
    all_to_all x1, blocking collectives, deliver(): lax.all_to_all(buffer, 'dom', split_axis=0, concat_axis=0, tiled=True)  12.1 us
    dot_general x8, matrix products, spread(): jnp.einsum('zdo,zmo->zdm', grouped_path_flow, link_path_incidence(grouped...  9.86 us
    gather x6, local copies, waits for them, and re-layouts, logit_split(): return demands[:, anchor_dest] * weight / weight_sum[:, anchor_dest]  8.92 us
    gather x4, local copies, waits for them, and re-layouts, logit_split(): weight = jnp.exp(-dispersion * (path_cost - lowest[:, anchor_dest]))  5.97 us
  transfers between devices with their start and end apart: 3, of which 3 were waited for; matrix products, arithmetic and copies ran while one was open for 3% of the time, Pallas kernels for 0%

commit v1 on v0

v1 whole, which is shorter than its diff:
```python
import functools

import jax
import jax.numpy as jnp
from jax import lax
from jax.experimental import pallas as pl
from jax.experimental.pallas import tpu as pltpu
from jax.sharding import PartitionSpec as P

ITERS = 2
MAX_RUN = 8
dispersion = 2.0
MESH = pl.DeviceIdType.MESH


def split3(value):
    high = value.astype(jnp.bfloat16)
    rest = value - high.astype(jnp.float32)
    mid = rest.astype(jnp.bfloat16)
    low = (rest - mid.astype(jnp.float32)).astype(jnp.bfloat16)
    return jnp.concatenate([high, mid, low], axis=0)


def join3(product):
    rows = product.shape[0] // 3
    return (product[2 * rows :] + product[rows : 2 * rows]) + product[:rows]


def offset(i, n):
    return n // 2 + (2 * (i % 2) - 1) * ((i + 1) // 2)


def kernel(
    n,
    m,
    x_ref,
    free_ref,
    cap_ref,
    demand_ref,
    od_ref,
    block_ref,
    count_ref,
    links_ref,
    tile_path_ref,
    load_ref,
    flow_ref,
    mean_ref,
    times,
    fsend,
    frecv,
    rsend,
    rrecv,
    incidence,
    factor,
    pick,
    masks,
    pair_demand,
    flow3,
    ens_buf,
    fs_sem,
    fr_sem,
    rs_sem,
    rr_sem,
    es_sem,
    er_sem,
):
    me = lax.axis_index("dom")
    ens = lax.axis_index("ens")
    scen = x_ref.shape[0]
    width = links_ref.shape[-1]
    hops = links_ref.shape[3]
    slots = links_ref.shape[2]
    link_blocks = x_ref.shape[1] // width
    paths = od_ref.shape[1]
    path_blocks = paths // width
    pairs = demand_ref.shape[1]

    barrier = pltpu.get_barrier_semaphore()
    for i in range(n - 1):
        pl.semaphore_signal(
            barrier, inc=1, device_id={"dom": lax.rem(me + 1 + i, n)}, device_id_type=MESH
        )
    for i in range(m - 1):
        pl.semaphore_signal(
            barrier, inc=1, device_id={"ens": lax.rem(ens + 1 + i, m)}, device_id_type=MESH
        )

    def forward_copy(j, src, dst, peer):
        return pltpu.make_async_remote_copy(
            src_ref=fsend.at[j, src],
            dst_ref=frecv.at[j, dst],
            send_sem=fs_sem.at[j, src],
            recv_sem=fr_sem.at[j, dst],
            device_id={"dom": peer},
            device_id_type=MESH,
        )

    def return_copy(j, src, dst, peer):
        return pltpu.make_async_remote_copy(
            src_ref=rsend.at[j, src],
            dst_ref=rrecv.at[j, dst],
            send_sem=rs_sem.at[j, src],
            recv_sem=rr_sem.at[j, dst],
            device_id={"dom": peer},
            device_id_type=MESH,
        )

    def ens_copy(dst, peer, slot):
        return pltpu.make_async_remote_copy(
            src_ref=ens_buf.at[ens],
            dst_ref=ens_buf.at[dst],
            send_sem=es_sem.at[slot],
            recv_sem=er_sem.at[dst],
            device_id={"ens": peer},
            device_id_type=MESH,
        )

    def bpr(g, value):
        loading = value / cap_ref[g : g + 1, :]
        square = loading * loading
        return free_ref[g : g + 1, :] * (1.0 + 0.15 * square * square)

    def tile_times(r, k):
        live = jnp.where(k < count_ref[0, r], 1.0, 0.0)
        return times[block_ref[0, k, r]] * live

    def send_times(j):
        def body(i, carry):
            r = lax.rem(me + offset(i, n), n)
            for k in range(slots):
                fsend[j, r, k] = tile_times(r, k)
            forward_copy(j, r, me, r).start()
            return carry

        lax.fori_loop(0, n - 1, body, 0)
        for k in range(slots):
            frecv[j, me, k] = tile_times(me, k)

    def fold_cost(j, s, acc):
        acc = list(acc)
        for k in range(slots):
            part = join3(
                jnp.dot(
                    split3(frecv[j, s, k]),
                    incidence[s * slots + k],
                    preferred_element_type=jnp.float32,
                )
            )
            for b in range(path_blocks):
                acc[b] = acc[b] + pick[s * slots + k, b : b + 1, :] * part
        return tuple(acc)

    def gather_cost(j):
        zero = jnp.zeros((scen, width), jnp.float32)
        acc = fold_cost(j, me, (zero,) * path_blocks)

        def body(i, acc):
            s = lax.rem(me - offset(n - 2 - i, n) + n, n)
            forward_copy(j, s, s, s).wait_recv()
            return fold_cost(j, s, acc)

        acc = lax.fori_loop(0, n - 1, body, acc)
        return jnp.concatenate(acc, axis=1)

    shifts = []
    step = 1
    while step < MAX_RUN:
        shifts.append(step)
        step *= 2

    def logit(cost):
        before, after = cost, cost
        for i, d in enumerate(shifts):
            before = jnp.where(
                masks[2 * i] > 0.0, jnp.minimum(before, pltpu.roll(before, d, 1)), before
            )
            after = jnp.where(
                masks[2 * i + 1] > 0.0, jnp.minimum(after, pltpu.roll(after, paths - d, 1)), after
            )
        weight = jnp.exp(-dispersion * (cost - jnp.minimum(before, after)))
        before, after = weight, weight
        for i, d in enumerate(shifts):
            before = before + masks[2 * i] * pltpu.roll(before, d, 1)
            after = after + masks[2 * i + 1] * pltpu.roll(after, paths - d, 1)
        return pair_demand[...] * weight / (before + (after - weight))

    def tile_flow(s, k):
        return join3(
            lax.dot_general(
                flow3[tile_path_ref[0, k, s]],
                incidence[s * slots + k],
                (((1,), (1,)), ((), ())),
                preferred_element_type=jnp.float32,
            )
        )

    def send_flows(j):
        def body(i, carry):
            s = lax.rem(me + offset(i, n), n)
            for k in range(slots):
                rsend[j, s, k] = tile_flow(s, k)
            return_copy(j, s, me, s).start()
            return carry

        lax.fori_loop(0, n - 1, body, 0)
        for k in range(slots):
            rrecv[j, me, k] = tile_flow(me, k)

    def fold_load(j, r, acc):
        acc = list(acc)
        for k in range(slots):
            tile = rrecv[j, r, k]
            for g in range(link_blocks):
                acc[g] = acc[g] + factor[r * slots + k, g : g + 1, :] * tile
        return tuple(acc)

    def gather_load(j):
        zero = jnp.zeros((scen, width), jnp.float32)
        acc = fold_load(j, me, (zero,) * link_blocks)

        def body(i, acc):
            r = lax.rem(me - offset(n - 2 - i, n) + n, n)
            return_copy(j, r, r, r).wait_recv()
            return fold_load(j, r, acc)

        return lax.fori_loop(0, n - 1, body, acc)

    def columns(g):
        return slice(g * width, (g + 1) * width)

    for g in range(link_blocks):
        times[g] = bpr(g, x_ref[:, columns(g)])
    pl.semaphore_wait(barrier, n + m - 2)
    send_times(0)

    rows = lax.broadcasted_iota(jnp.int32, (width, width), 0)
    link_ids = lax.broadcasted_iota(jnp.int32, (link_blocks, width), 0)
    path_ids = lax.broadcasted_iota(jnp.int32, (path_blocks, width), 0)

    def tables(s, carry):
        for k in range(slots):
            t = s * slots + k
            links = links_ref[0, s, k]
            count = jnp.zeros((width, width), jnp.float32)
            for h in range(hops):
                count = count + jnp.where(links[h : h + 1, :] == rows, 1.0, 0.0)
            incidence[t] = count.astype(jnp.bfloat16)
            pick[t] = jnp.where(path_ids == tile_path_ref[0, k, s], 1.0, 0.0)
            live = jnp.where(k < count_ref[0, s], 1.0, 0.0)
            factor[t] = jnp.where(link_ids == block_ref[0, k, s], 1.0, 0.0) * live
        return carry

    lax.fori_loop(0, n, tables, 0)
    od = jnp.broadcast_to(od_ref[...], (scen, paths))
    for i, d in enumerate(shifts):
        masks[2 * i] = jnp.where(pltpu.roll(od, d, 1) == od, 1.0, 0.0)
        masks[2 * i + 1] = jnp.where(pltpu.roll(od, paths - d, 1) == od, 1.0, 0.0)
    demand3 = split3(demand_ref[...])
    pair_ids = lax.broadcasted_iota(jnp.int32, (pairs, width), 0)
    for b in range(path_blocks):
        chosen = jnp.where(od_ref[:, columns(b)] == pair_ids, 1.0, 0.0).astype(jnp.bfloat16)
        pair_demand[:, columns(b)] = join3(
            jnp.dot(demand3, chosen, preferred_element_type=jnp.float32)
        )

    current_ref = x_ref
    for j in range(ITERS):
        if j > 0:
            send_times(j)
        flow = logit(gather_cost(j))
        if j == ITERS - 1:
            flow_ref[...] = flow
        for b in range(path_blocks):
            flow3[b] = split3(flow[:, columns(b)])
        send_flows(j)
        loads = gather_load(j)
        for g in range(link_blocks):
            current = current_ref[:, columns(g)]
            current = current + (loads[g] - current) / (j + 2.0)
            load_ref[:, columns(g)] = current
            link_time = bpr(g, current)
            if j < ITERS - 1:
                times[g] = link_time
            else:
                ens_buf[ens, g : g + 1, :] = jnp.sum(link_time, axis=0, keepdims=True)
        current_ref = load_ref

    for i in range(1, m):
        ens_copy(ens, lax.rem(ens + i, m), i).start()
    for j in range(ITERS):

        def drain(i, carry):
            r = lax.rem(me + offset(i, n), n)
            forward_copy(j, r, me, r).wait_send()
            return_copy(j, r, me, r).wait_send()
            return carry

        lax.fori_loop(0, n - 1, drain, 0)
    for i in range(1, m):
        peer = lax.rem(ens + m - i, m)
        ens_copy(peer, peer, i).wait_recv()
    total = ens_buf[0]
    for i in range(1, m):
        total = total + ens_buf[i]
    mean_ref[...] = total / (scen * m)
    for i in range(1, m):
        ens_copy(ens, lax.rem(ens + i, m), i).wait_send()


def local(
    n,
    m,
    link_flow,
    free_time,
    capacity,
    demand,
    path_od,
    send_blocks,
    send_counts,
    tile_links,
    tile_paths,
):
    scen, links = link_flow.shape
    width = tile_links.shape[-1]
    slots = tile_links.shape[2]
    tiles = n * slots
    link_blocks = links // width
    paths = path_od.shape[1]
    path_blocks = paths // width
    pairs = demand.shape[2]
    f32 = jnp.float32
    mask_count = 2 * max(1, (MAX_RUN - 1).bit_length())
    exchange = pltpu.VMEM((ITERS, n, slots, scen, width), f32)
    vmem = pl.BlockSpec(memory_space=pltpu.VMEM)
    smem = pl.BlockSpec(memory_space=pltpu.SMEM)
    load, flow, mean = pl.pallas_call(
        functools.partial(kernel, n, m),
        out_shape=(
            jax.ShapeDtypeStruct((scen, links), f32),
            jax.ShapeDtypeStruct((scen, paths), f32),
            jax.ShapeDtypeStruct((link_blocks, width), f32),
        ),
        in_specs=[vmem, vmem, vmem, vmem, vmem, smem, smem, vmem, smem],
        out_specs=(vmem, vmem, vmem),
        scratch_shapes=[
            pltpu.VMEM((link_blocks, scen, width), f32),
            exchange,
            exchange,
            exchange,
            exchange,
            pltpu.VMEM((tiles, width, width), jnp.bfloat16),
            pltpu.VMEM((tiles, link_blocks, width), f32),
            pltpu.VMEM((tiles, path_blocks, width), f32),
            pltpu.VMEM((mask_count, scen, paths), f32),
            pltpu.VMEM((scen, paths), f32),
            pltpu.VMEM((path_blocks, 3 * scen, width), jnp.bfloat16),
            pltpu.VMEM((m, link_blocks, width), f32),
            pltpu.SemaphoreType.DMA((ITERS, n)),
            pltpu.SemaphoreType.DMA((ITERS, n)),
            pltpu.SemaphoreType.DMA((ITERS, n)),
            pltpu.SemaphoreType.DMA((ITERS, n)),
            pltpu.SemaphoreType.DMA((m,)),
            pltpu.SemaphoreType.DMA((m,)),
        ],
        compiler_params=pltpu.CompilerParams(
            collective_id=0, has_side_effects=True, vmem_limit_bytes=56 * 1024 * 1024
        ),
        name="equilibrium",
    )(
        link_flow,
        free_time.reshape(link_blocks, width),
        capacity.reshape(link_blocks, width),
        demand.reshape(scen, pairs),
        path_od,
        jnp.swapaxes(send_blocks, 1, 2),
        send_counts,
        tile_links,
        jnp.swapaxes(tile_paths, 1, 2),
    )
    return load, flow, mean.reshape(links)


def solution(mesh):
    in_specs = (
        P("ens", "dom"),
        P("dom"),
        P("dom"),
        P("ens", "dom", None),
        P("dom", None),
        P("dom", None, None),
        P("dom", None),
        P("dom", None, None, None, None),
        P("dom", None, None),
    )
    out_specs = (P("ens", "dom"), P("ens", "dom"), P("dom"))
    body = functools.partial(local, mesh.shape["dom"], mesh.shape["ens"])
    return jax.shard_map(body, mesh=mesh, in_specs=in_specs, out_specs=out_specs, check_vma=False)
```

time: 130 us -> 46.6 us (0.36)
  Pallas kernels: 0 us -> 41.5 us
  other arithmetic: 36.4 us -> 0 us
  waiting for transfers between devices: 21.6 us -> 0 us
  blocking collectives: 17.8 us -> 0 us
  matrix products: 17 us -> 0 us
  local copies, waits for them, and re-layouts: 20.5 us -> 4.22 us
  starting transfers between devices: 14.4 us -> 0 us
    pallas_call x0 -> x1, Pallas kernels: none -> 41.5 us  [local(): pl.pallas_call(functools.partial(kernel, n, m), out_shape=(jax.ShapeDtype...]
    all_to_all x3 -> x0, waiting for transfers between devices: 21.6 us -> none  [deliver(): lax.all_to_all(buffer, 'dom', split_axis=0, concat_axis=0, tiled=True)]
    gather x14 -> x0, local copies, waits for them, and re-layouts: 17.2 us -> none  [the longest x6 8.92 us: logit_split(): return demands[:, anchor_dest] * weight / weight_sum[:, anchor_dest]]
    dot_general x26 -> x0, matrix products: 17 us -> none  [the longest x8 9.86 us: spread(): jnp.einsum('zdo,zmo->zdm', grouped_path_flow, link_path_incidence(grouped...]
    all_to_all x3 -> x0, starting transfers between devices: 14.4 us -> none  [deliver(): lax.all_to_all(buffer, 'dom', split_axis=0, concat_axis=0, tiled=True)]
    another operation x2 -> x0, other arithmetic: 13.1 us -> none  [logit_split(): lowest = jnp.full((path_cost.shape[0], pair_count), jnp.inf, path_cost.dt...]
    scatter-add x2 -> x0, other arithmetic: 13.1 us -> none  [logit_split(): jnp.zeros((path_cost.shape[0], pair_count), path_cost.dtype)]
    all_to_all x1 -> x0, blocking collectives: 12.1 us -> none  [deliver(): lax.all_to_all(buffer, 'dom', split_axis=0, concat_axis=0, tiled=True)]
  transfers between devices with their start and end apart: 3 -> 0, of which waited for: 3 -> 0; matrix products, arithmetic and copies ran while one was open for 3% -> 0% of each run, Pallas kernels for 0% -> 0%
where the time goes in v1:
time: 46.6 us; the launch traced here: 46.3 us
  Pallas kernels  41.5 us (89%)
  local copies, waits for them, and re-layouts  4.22 us (9%)
  between operations  0.65 us (1%)
    pallas_call x1, Pallas kernels, local(): pl.pallas_call(functools.partial(kernel, n, m), out_shape=(jax.ShapeDtype...  41.5 us
    unnamed x8, local copies, waits for them, and re-layouts  4.22 us

profile of v1, /device:TPU:0, one launch (start us, length us, event | category | flops | bytes accessed | tf_op | source)
XLA Modules:
  0.0 46.3 jit_solution(15870652847203145376)
XLA Ops:
  0.6 1.3 %copy.14 = f32[16,1,256]{2,0,1:T(8,128)} copy(f32[16,1,256]{2,1,0:T(1,128)} %param.12) | data formatting | bytes 32768
  2.0 41.5 %equilibrium.1 = (f32[16,2048]{1,0:T(8,128)}, f32[16,1024]{1,0:T(8,128)}, f32[16,128]{1,0:T(8,128)}) custom-call(f32[16,2048]{1,0:T(8,128)} %x_ref.1, f32[16,128]{1,0:T(8,128)} %bitcast.10, f32[16,128]{1,0:T(8,128)} %bitcast.11, f32[16,256]{1,0:T(8,128)} %bitcast.8, s32[1,1024]{1,0:T(1,128)} %od_ref.1, s32[1,4,8]{2,1,0:T(4,128)} %bitcast.12, ...), custom_call_target="tpu_custom_call" | custom-call | tf_op jit(solution)/shard_map/equilibrium/pallas_call | solution.py:336
  43.4 0.0 copy-start
  43.4 1.6 %copy.18 = f32[16,2048]{1,0:T(8,128)} copy(f32[16,2048]{1,0:T(8,128)} %get-tuple-element.12) | data formatting | bytes 262144
  45.0 0.0 copy-done
  45.0 0.0 copy-start.1
  45.0 0.6 %copy.19 = f32[16,1024]{1,0:T(8,128)} copy(f32[16,1024]{1,0:T(8,128)S(1)} %copy-done) | data formatting | bytes 131072
  45.7 0.1 copy-done.1
  45.7 0.6 %copy.20 = f32[2048]{0:T(1024)} copy(f32[2048]{0:T(1024)S(1)} %bitcast.9) | data formatting | bytes 16384
Async XLA Ops:
  43.4 1.6 %copy-start = (f32[16,1024]{1,0:T(8,128)S(1)}, f32[16,1024]{1,0:T(8,128)}, u32[]{:S(2)}) copy-start(f32[16,1024]{1,0:T(8,128)} %get-tuple-element.13) | copy-start | bytes 196612
  45.0 0.7 %copy-start.1 = (f32[16,128]{1,0:T(8,128)S(1)}, f32[16,128]{1,0:T(8,128)}, u32[]{:S(2)}) copy-start(f32[16,128]{1,0:T(8,128)} %get-tuple-element.8) | copy-start | bytes 24580

commit v2 on v1

--- a/solution.py
+++ b/solution.py
@@ -14,11 +14,10 @@
 
 
 def split3(value):
-    high = value.astype(jnp.bfloat16)
-    rest = value - high.astype(jnp.float32)
-    mid = rest.astype(jnp.bfloat16)
-    low = (rest - mid.astype(jnp.float32)).astype(jnp.bfloat16)
-    return jnp.concatenate([high, mid, low], axis=0)
+    high = value.astype(jnp.bfloat16).astype(jnp.float32)
+    rest = value - high
+    mid = rest.astype(jnp.bfloat16).astype(jnp.float32)
+    return jnp.concatenate([high, mid, rest - mid], axis=0).astype(jnp.bfloat16)
 
 
 def join3(product):
@@ -26,13 +25,34 @@
     return (product[2 * rows :] + product[rows : 2 * rows]) + product[:rows]
 
 
-def offset(i, n):
-    return n // 2 + (2 * (i % 2) - 1) * ((i + 1) // 2)
+def partner(me, i, n):
+    step = n - 1 - i
+    if n & (n - 1):
+        return lax.rem(me + step, n)
+    other = 0
+    bit = 1
+    while bit < n:
+        other = other + lax.rem(me // bit + step // bit, 2) * bit
+        bit *= 2
+    return other
 
 
 def kernel(
     n,
     m,
+    streams,
+    x_hbm,
+    free_hbm,
+    cap_hbm,
+    demand_hbm,
+    od_hbm,
+    block_hbm,
+    count_hbm,
+    links_hbm,
+    tile_path_hbm,
+    load_hbm,
+    flow_hbm,
+    mean_hbm,
     x_ref,
     free_ref,
     cap_ref,
@@ -45,6 +65,8 @@
     load_ref,
     flow_ref,
     mean_ref,
+    in_sem,
+    out_sem,
     times,
     fsend,
     frecv,
@@ -66,14 +88,14 @@
 ):
     me = lax.axis_index("dom")
     ens = lax.axis_index("ens")
-    scen = x_ref.shape[0]
+    scen = x_ref.shape[0] // streams
     width = links_ref.shape[-1]
     hops = links_ref.shape[3]
     slots = links_ref.shape[2]
     link_blocks = x_ref.shape[1] // width
     paths = od_ref.shape[1]
     path_blocks = paths // width
-    pairs = demand_ref.shape[1]
+    pairs = demand_ref.shape[2]
 
     barrier = pltpu.get_barrier_semaphore()
     for i in range(n - 1):
@@ -84,6 +106,23 @@
         pl.semaphore_signal(
             barrier, inc=1, device_id={"ens": lax.rem(ens + 1 + i, m)}, device_id_type=MESH
         )
+
+    staged = (
+        (x_hbm, x_ref),
+        (free_hbm, free_ref),
+        (cap_hbm, cap_ref),
+        (block_hbm, block_ref),
+        (count_hbm, count_ref),
+        (links_hbm, links_ref),
+        (tile_path_hbm, tile_path_ref),
+        (od_hbm, od_ref),
+        (demand_hbm, demand_ref),
+    )
+    staging = [
+        pltpu.make_async_copy(src, dst, in_sem.at[i]) for i, (src, dst) in enumerate(staged)
+    ]
+    for copy in staging:
+        copy.start()
 
     def forward_copy(j, src, dst, peer):
         return pltpu.make_async_remote_copy(
@@ -120,21 +159,21 @@
         square = loading * loading
         return free_ref[g : g + 1, :] * (1.0 + 0.15 * square * square)
 
-    def tile_times(r, k):
+    def tile_times(h, r, k):
         live = jnp.where(k < count_ref[0, r], 1.0, 0.0)
-        return times[block_ref[0, k, r]] * live
-
-    def send_times(j):
+        return times[h * link_blocks + block_ref[0, k, r]] * live
+
+    def send_times(h, j):
         def body(i, carry):
-            r = lax.rem(me + offset(i, n), n)
+            r = partner(me, i, n)
             for k in range(slots):
-                fsend[j, r, k] = tile_times(r, k)
+                fsend[j, r, k] = tile_times(h, r, k)
             forward_copy(j, r, me, r).start()
             return carry
 
-        lax.fori_loop(0, n - 1, body, 0)
+        lax.fori_loop(0, n - 1, body, 0, unroll=n <= 8)
         for k in range(slots):
-            frecv[j, me, k] = tile_times(me, k)
+            frecv[j, me, k] = tile_times(h, me, k)
 
     def fold_cost(j, s, acc):
         acc = list(acc)
@@ -155,11 +194,11 @@
         acc = fold_cost(j, me, (zero,) * path_blocks)
 
         def body(i, acc):
-            s = lax.rem(me - offset(n - 2 - i, n) + n, n)
+            s = partner(me, i, n)
             forward_copy(j, s, s, s).wait_recv()
             return fold_cost(j, s, acc)
 
-        acc = lax.fori_loop(0, n - 1, body, acc)
+        acc = lax.fori_loop(0, n - 1, body, acc, unroll=n <= 8)
         return jnp.concatenate(acc, axis=1)
 
     shifts = []
@@ -168,7 +207,10 @@
         shifts.append(step)
         step *= 2
 
-    def logit(cost):
+    def rows_of(h):
+        return slice(h * scen, (h + 1) * scen)
+
+    def logit(h, cost):
         before, after = cost, cost
         for i, d in enumerate(shifts):
             before = jnp.where(
@@ -182,29 +224,29 @@
         for i, d in enumerate(shifts):
             before = before + masks[2 * i] * pltpu.roll(before, d, 1)
             after = after + masks[2 * i + 1] * pltpu.roll(after, paths - d, 1)
-        return pair_demand[...] * weight / (before + (after - weight))
-
-    def tile_flow(s, k):
+        return pair_demand[rows_of(h), :] * weight / (before + (after - weight))
+
+    def tile_flow(h, s, k):
         return join3(
             lax.dot_general(
-                flow3[tile_path_ref[0, k, s]],
+                flow3[h * path_blocks + tile_path_ref[0, k, s]],
                 incidence[s * slots + k],
                 (((1,), (1,)), ((), ())),
                 preferred_element_type=jnp.float32,
             )
         )
 
-    def send_flows(j):
+    def send_flows(h, j):
         def body(i, carry):
-            s = lax.rem(me + offset(i, n), n)
+            s = partner(me, i, n)
             for k in range(slots):
-                rsend[j, s, k] = tile_flow(s, k)
+                rsend[j, s, k] = tile_flow(h, s, k)
             return_copy(j, s, me, s).start()
             return carry
 
-        lax.fori_loop(0, n - 1, body, 0)
+        lax.fori_loop(0, n - 1, body, 0, unroll=n <= 8)
         for k in range(slots):
-            rrecv[j, me, k] = tile_flow(me, k)
+            rrecv[j, me, k] = tile_flow(h, me, k)
 
     def fold_load(j, r, acc):
         acc = list(acc)
@@ -219,19 +261,25 @@
         acc = fold_load(j, me, (zero,) * link_blocks)
 
         def body(i, acc):
-            r = lax.rem(me - offset(n - 2 - i, n) + n, n)
+            r = partner(me, i, n)
             return_copy(j, r, r, r).wait_recv()
             return fold_load(j, r, acc)
 
-        return lax.fori_loop(0, n - 1, body, acc)
+        return lax.fori_loop(0, n - 1, body, acc, unroll=n <= 8)
 
     def columns(g):
         return slice(g * width, (g + 1) * width)
 
-    for g in range(link_blocks):
-        times[g] = bpr(g, x_ref[:, columns(g)])
+    for copy in staging[:5]:
+        copy.wait()
+    for h in range(streams):
+        for g in range(link_blocks):
+            times[h * link_blocks + g] = bpr(g, x_ref[rows_of(h), columns(g)])
     pl.semaphore_wait(barrier, n + m - 2)
-    send_times(0)
+    for h in range(streams):
+        send_times(h, h)
+    for copy in staging[5:]:
+        copy.wait()
 
     rows = lax.broadcasted_iota(jnp.int32, (width, width), 0)
     link_ids = lax.broadcasted_iota(jnp.int32, (link_blocks, width), 0)
@@ -255,7 +303,7 @@
     for i, d in enumerate(shifts):
         masks[2 * i] = jnp.where(pltpu.roll(od, d, 1) == od, 1.0, 0.0)
         masks[2 * i + 1] = jnp.where(pltpu.roll(od, paths - d, 1) == od, 1.0, 0.0)
-    demand3 = split3(demand_ref[...])
+    demand3 = split3(demand_ref[:, 0, :])
     pair_ids = lax.broadcasted_iota(jnp.int32, (pairs, width), 0)
     for b in range(path_blocks):
         chosen = jnp.where(od_ref[:, columns(b)] == pair_ids, 1.0, 0.0).astype(jnp.bfloat16)
@@ -263,48 +311,79 @@
             jnp.dot(demand3, chosen, preferred_element_type=jnp.float32)
         )
 
+    flow_copy = pltpu.make_async_copy(flow_ref, flow_hbm, out_sem.at[0])
+    load_copy = pltpu.make_async_copy(load_ref, load_hbm, out_sem.at[1])
+    mean_copy = pltpu.make_async_copy(mean_ref, mean_hbm, out_sem.at[2])
     current_ref = x_ref
     for j in range(ITERS):
-        if j > 0:
-            send_times(j)
-        flow = logit(gather_cost(j))
-        if j == ITERS - 1:
-            flow_ref[...] = flow
-        for b in range(path_blocks):
-            flow3[b] = split3(flow[:, columns(b)])
-        send_flows(j)
-        loads = gather_load(j)
-        for g in range(link_blocks):
-            current = current_ref[:, columns(g)]
-            current = current + (loads[g] - current) / (j + 2.0)
-            load_ref[:, columns(g)] = current
-            link_time = bpr(g, current)
-            if j < ITERS - 1:
-                times[g] = link_time
-            else:
-                ens_buf[ens, g : g + 1, :] = jnp.sum(link_time, axis=0, keepdims=True)
+        last = j == ITERS - 1
+        for h in range(streams):
+            phase = j * streams + h
+            flow = logit(h, gather_cost(phase))
+            if last:
+                flow_ref[rows_of(h), :] = flow
+            for b in range(path_blocks):
+                flow3[h * path_blocks + b] = split3(flow[:, columns(b)])
+            send_flows(h, phase)
+        if last:
+            flow_copy.start()
+        for h in range(streams):
+            phase = j * streams + h
+            loads = gather_load(phase)
+            for g in range(link_blocks):
+                current = current_ref[rows_of(h), columns(g)]
+                current = current + (loads[g] - current) / (j + 2.0)
+                load_ref[rows_of(h), columns(g)] = current
+                link_time = bpr(g, current)
+                if not last:
+                    times[h * link_blocks + g] = link_time
+                else:
+                    summed = jnp.sum(link_time, axis=0, keepdims=True)
+                    if h > 0:
+                        summed = summed + ens_buf[ens, g : g + 1, :]
+                    ens_buf[ens, g : g + 1, :] = summed
+            if not last:
+                send_times(h, phase + streams)
         current_ref = load_ref
 
     for i in range(1, m):
         ens_copy(ens, lax.rem(ens + i, m), i).start()
-    for j in range(ITERS):
-
-        def drain(i, carry):
-            r = lax.rem(me + offset(i, n), n)
-            forward_copy(j, r, me, r).wait_send()
-            return_copy(j, r, me, r).wait_send()
-            return carry
-
-        lax.fori_loop(0, n - 1, drain, 0)
+    load_copy.start()
+
+    def drain(i, carry):
+        r = partner(me, i, n)
+        for phase in range(ITERS * streams):
+            forward_copy(phase, r, me, r).wait_send()
+            return_copy(phase, r, me, r).wait_send()
+        return carry
+
+    lax.fori_loop(0, n - 1, drain, 0)
     for i in range(1, m):
         peer = lax.rem(ens + m - i, m)
         ens_copy(peer, peer, i).wait_recv()
     total = ens_buf[0]
     for i in range(1, m):
         total = total + ens_buf[i]
-    mean_ref[...] = total / (scen * m)
+    mean_ref[...] = total / (x_ref.shape[0] * m)
+    mean_copy.start()
     for i in range(1, m):
         ens_copy(ens, lax.rem(ens + i, m), i).wait_send()
+    flow_copy.wait()
+    load_copy.wait()
+    mean_copy.wait()
+
+
+def finish(a, b, c, oa, ob, oc, va, vb, vc, in_sem, out_sem):
+    triples = ((a, va, oa), (b, vb, ob), (c, vc, oc))
+    loads = [pltpu.make_async_copy(s, v, in_sem.at[i]) for i, (s, v, _) in enumerate(triples)]
+    stores = [pltpu.make_async_copy(v, o, out_sem.at[i]) for i, (_, v, o) in enumerate(triples)]
+    for copy in loads:
+        copy.start()
+    for load, store in zip(loads, stores):
+        load.wait()
+        store.start()
+    for copy in stores:
+        copy.wait()
 
 
 def local(
@@ -330,20 +409,37 @@
     pairs = demand.shape[2]
     f32 = jnp.float32
     mask_count = 2 * max(1, (MAX_RUN - 1).bit_length())
-    exchange = pltpu.VMEM((ITERS, n, slots, scen, width), f32)
-    vmem = pl.BlockSpec(memory_space=pltpu.VMEM)
-    smem = pl.BlockSpec(memory_space=pltpu.SMEM)
+    streams = 1
+    phases = ITERS * streams
+    part = scen // streams
+    exchange = pltpu.VMEM((phases, n, slots, part, width), f32)
+    stay = pl.BlockSpec(memory_space=pl.ANY)
+    i32 = jnp.int32
     load, flow, mean = pl.pallas_call(
-        functools.partial(kernel, n, m),
+        functools.partial(kernel, n, m, streams),
         out_shape=(
             jax.ShapeDtypeStruct((scen, links), f32),
             jax.ShapeDtypeStruct((scen, paths), f32),
             jax.ShapeDtypeStruct((link_blocks, width), f32),
         ),
-        in_specs=[vmem, vmem, vmem, vmem, vmem, smem, smem, vmem, smem],
-        out_specs=(vmem, vmem, vmem),
+        in_specs=[stay] * 9,
+        out_specs=(stay, stay, stay),
         scratch_shapes=[
-            pltpu.VMEM((link_blocks, scen, width), f32),
+            pltpu.VMEM((scen, links), f32),
+            pltpu.VMEM((link_blocks, width), f32),
+            pltpu.VMEM((link_blocks, width), f32),
+            pltpu.VMEM((scen, 1, pairs), f32),
+            pltpu.VMEM((1, paths), i32),
+            pltpu.SMEM((1, slots, n), i32),
+            pltpu.SMEM((1, n), i32),
+            pltpu.VMEM(tile_links.shape, i32),
+            pltpu.SMEM((1, slots, n), i32),
+            pltpu.VMEM((scen, links), f32),
+            pltpu.VMEM((scen, paths), f32),
+            pltpu.VMEM((link_blocks, width), f32),
+            pltpu.SemaphoreType.DMA((9,)),
+            pltpu.SemaphoreType.DMA((3,)),
+            pltpu.VMEM((streams * link_blocks, part, width), f32),
             exchange,
             exchange,
             exchange,
@@ -351,14 +447,14 @@
             pltpu.VMEM((tiles, width, width), jnp.bfloat16),
             pltpu.VMEM((tiles, link_blocks, width), f32),
             pltpu.VMEM((tiles, path_blocks, width), f32),
-            pltpu.VMEM((mask_count, scen, paths), f32),
+            pltpu.VMEM((mask_count, part, paths), f32),
             pltpu.VMEM((scen, paths), f32),
-            pltpu.VMEM((path_blocks, 3 * scen, width), jnp.bfloat16),
+            pltpu.VMEM((streams * path_blocks, 3 * part, width), jnp.bfloat16),
             pltpu.VMEM((m, link_blocks, width), f32),
-            pltpu.SemaphoreType.DMA((ITERS, n)),
-            pltpu.SemaphoreType.DMA((ITERS, n)),
-            pltpu.SemaphoreType.DMA((ITERS, n)),
-            pltpu.SemaphoreType.DMA((ITERS, n)),
+            pltpu.SemaphoreType.DMA((phases, n)),
+            pltpu.SemaphoreType.DMA((phases, n)),
+            pltpu.SemaphoreType.DMA((phases, n)),
+            pltpu.SemaphoreType.DMA((phases, n)),
             pltpu.SemaphoreType.DMA((m,)),
             pltpu.SemaphoreType.DMA((m,)),
         ],
@@ -370,13 +466,31 @@
         link_flow,
         free_time.reshape(link_blocks, width),
         capacity.reshape(link_blocks, width),
-        demand.reshape(scen, pairs),
+        demand,
         path_od,
         jnp.swapaxes(send_blocks, 1, 2),
         send_counts,
         tile_links,
         jnp.swapaxes(tile_paths, 1, 2),
     )
+    load, flow, mean = pl.pallas_call(
+        finish,
+        out_shape=(
+            jax.ShapeDtypeStruct((scen, links), f32),
+            jax.ShapeDtypeStruct((scen, paths), f32),
+            jax.ShapeDtypeStruct((link_blocks, width), f32),
+        ),
+        in_specs=[stay] * 3,
+        out_specs=(stay,) * 3,
+        scratch_shapes=[
+            pltpu.VMEM((scen, links), f32),
+            pltpu.VMEM((scen, paths), f32),
+            pltpu.VMEM((link_blocks, width), f32),
+            pltpu.SemaphoreType.DMA((3,)),
+            pltpu.SemaphoreType.DMA((3,)),
+        ],
+        name="finish",
+    )(load, flow, mean)
     return load, flow, mean.reshape(links)
 
 

time: 46.6 us -> 40.1 us (0.86)
  local copies, waits for them, and re-layouts: 4.22 us -> 0 us
  Pallas kernels: 41.5 us -> 39.3 us
    unnamed x8 -> x0, local copies, waits for them, and re-layouts: 4.22 us -> none
    pallas_call x1 -> x2, Pallas kernels: 41.5 us -> 39.3 us  [the longest x1 37.7 us: local(): pl.pallas_call(functools.partial(kernel, n, m, streams), out_shape=(jax.S...]
where the time goes in v2:
time: 40.1 us; the launch traced here: 40 us
  Pallas kernels  39.3 us (98%)
  between operations  0.64 us (2%)
    pallas_call x1, Pallas kernels, local(): pl.pallas_call(functools.partial(kernel, n, m, streams), out_shape=(jax.S...  37.7 us
    pallas_call x1, Pallas kernels, local(): pl.pallas_call(finish, out_shape=(jax.ShapeDtypeStruct((scen, links), f32...  1.63 us

profile of v2, /device:TPU:0, one launch (start us, length us, event | category | flops | bytes accessed | tf_op | source)
XLA Modules:
  0.0 40.0 jit_solution(1974255106436518099)
XLA Ops:
  0.6 37.7 %equilibrium.1 = (f32[16,2048]{1,0:T(8,128)}, f32[16,1024]{1,0:T(8,128)}, f32[16,128]{1,0:T(8,128)}) custom-call(f32[16,2048]{1,0:T(8,128)} %x_hbm.1, f32[16,128]{1,0:T(8,128)} %bitcast.5, f32[16,128]{1,0:T(8,128)} %bitcast.6, f32[16,1,256]{2,1,0:T(1,128)} %demand_hbm.1, s32[1,1024]{1,0:T(1,128)} %od_hbm.1, s32[1,4,8]{2,1,0:T(4,128)} %bitcast.7, ...), custom_call_target="tpu_custom_call" | custom-call | tf_op jit(solution)/shard_map/equilibrium/pallas_call | solution.py:418
  38.3 1.6 %finish.1 = (f32[16,2048]{1,0:T(8,128)}, f32[16,1024]{1,0:T(8,128)}, f32[16,128]{1,0:T(8,128)}) custom-call(f32[16,2048]{1,0:T(8,128)} %get-tuple-element.9.a, f32[16,1024]{1,0:T(8,128)} %get-tuple-element.10.b, f32[16,128]{1,0:T(8,128)} %get-tuple-element.11.c), custom_call_target="tpu_custom_call" | custom-call | tf_op jit(solution)/shard_map/finish/pallas_call | solution.py:476
